TPU v7x, 512 devices: a whole 4x4x16 slice. The times are simulated.
512 devices in a mesh: grp: 16 (over z), voc: 32 (over x, y, core).
Axes of the slice: x: 4, y: 4, z: 16, core: 2. Of those that a mesh axis runs over, the one named last changes fastest.
Arguments:
- hidden_states: bfloat16 [16384, 8192], P('grp', 'voc'), may hold values from -6 to 6
- target_logits: float32 [16384, 16384], P('grp', 'voc'), may hold values from -12 to 240
- labels: int32 [16384, 8], P('grp'), may hold values from 0 to 2047
- down_weight: bfloat16 [8192, 256], P('voc'), may hold values from -0.0625 to 0.0625
- up_weight: bfloat16 [256, 8192], P(None, 'grp'), may hold values from -0.75 to 0.75
- head_weight: bfloat16 [8192, 16384], P('grp', 'voc'), may hold values from -0.0625 to 0.0625
Outputs:
- frame_loss: float32 [32, 16, 256], P('voc', 'grp')
- grad_a: float32 [8192, 256], P('voc')
- grad_b: float32 [256, 8192], P(None, 'grp')
All inputs are finite; a program needn't handle non-finite values.
Results may differ from a plain program's by a relative error of at most 0.0046.
Values may be sent and summed in bfloat16 or wider, within the bound.
A program may use at most 64 MiB of HBM per device.

v0:
```python
import jax
import jax.numpy as jnp
from jax import lax
from jax.sharding import PartitionSpec as P

HEAD = 2
LAM = 0.1


def passed_along(block, axis, distance):
    devices = range(lax.axis_size(axis))
    route = [(i - distance, i) for i in devices if i - distance in devices]
    return lax.ppermute(block, axis, route)


def partner(value, axis, bit):
    mask = 2**bit
    pairs = [(source, source ^ mask) for source in range(lax.axis_size(axis))]
    return lax.ppermute(value, axis, pairs)


def silu_slope(values):
    sigma = jax.nn.sigmoid(values)
    return sigma * (1.0 + values * (1.0 - sigma))


def log_normalize(values):
    top_value = jnp.max(values, -1, keepdims=True)
    return values - top_value - jnp.log(jnp.sum(jnp.exp(values - top_value), -1, keepdims=True))


def inner_rows(left, right):
    return lax.dot_general(
        left, right, (((0,), (0,)), ((), ())), preferred_element_type=jnp.float32
    )


def inner_cols(left, right):
    return lax.dot_general(
        left, right, (((1,), (1,)), ((), ())), preferred_element_type=jnp.float32
    )


def regroup(blocks, bit_total, swapper):
    position = lax.axis_index("voc")
    for bit_number in range(bit_total):
        leading = blocks.shape[:-3]
        slot_count = blocks.shape[-3]
        lower_count = 1 << bit_number
        upper_count = slot_count // (2 * lower_count)
        viewed = blocks.reshape(leading + (upper_count, 2, lower_count) + blocks.shape[-2:])
        bit_axis = len(leading) + 1
        own_bit = position // lower_count % 2
        zero_half = lax.index_in_dim(viewed, 0, bit_axis, keepdims=False)
        one_half = lax.index_in_dim(viewed, 1, bit_axis, keepdims=False)
        kept = jnp.where(own_bit == 0, zero_half, one_half)
        outgoing = jnp.where(own_bit == 0, one_half, zero_half)
        arrived = swapper(outgoing, bit_number)
        low_half = jnp.where(own_bit == 0, kept, arrived)
        high_half = jnp.where(own_bit == 0, arrived, kept)
        blocks = jnp.stack((low_half, high_half), bit_axis).reshape(blocks.shape)
    return blocks


def on_device(hidden_states, target_logits, labels, down_weight, up_weight, head_weight):
    row_count, slice_cols = target_logits.shape
    book_count = labels.shape[1]
    group_count = lax.axis_size("grp")
    per_book = lax.axis_size("voc") // book_count
    bit_total = per_book.bit_length() - 1
    book_width = slice_cols * per_book
    block_rows = row_count // per_book
    position = lax.axis_index("voc")
    book_index = position // per_book
    book_part = position % per_book
    pre_act = lax.psum(
        jnp.dot(hidden_states, down_weight, preferred_element_type=jnp.float32), "voc"
    )
    activation = jax.nn.silu(pre_act).astype(jnp.bfloat16)
    vocab_proj = lax.psum(
        jnp.dot(up_weight, head_weight, preferred_element_type=jnp.float32), "grp"
    ).astype(jnp.bfloat16)
    draft_logits = target_logits + jnp.dot(
        activation, vocab_proj, preferred_element_type=jnp.float32
    )
    incoming = passed_along(target_logits[:HEAD], "grp", -1)
    shifted = jnp.concatenate((target_logits[HEAD:], incoming), 0)
    frame_index = lax.axis_index("grp") * row_count + jnp.arange(row_count)
    live_mask = (frame_index < row_count * group_count - HEAD).astype(jnp.float32)
    paired = jnp.stack((shifted, draft_logits)).reshape(2, per_book, block_rows, slice_cols)
    regrouped = regroup(
        paired, bit_total, lambda piece_data, bit_number: partner(piece_data, "voc", bit_number)
    )
    regrouped = regrouped.transpose(0, 2, 1, 3).reshape(2, block_rows, book_width)
    log_target = log_normalize(regrouped[0])
    log_draft = log_normalize(regrouped[1])
    block_start = book_part * block_rows
    label_ids = lax.dynamic_slice(labels, (block_start, book_index), (block_rows, 1))[:, 0]
    live_rows = lax.dynamic_slice_in_dim(live_mask, block_start, block_rows)
    onehot = (jnp.arange(book_width)[None, :] == label_ids[:, None]).astype(jnp.float32)
    target_prob = jnp.exp(log_target)
    draft_prob = jnp.exp(log_draft)
    divergence = jnp.sum(target_prob * (log_target - log_draft), -1)
    picked = jnp.sum(onehot * log_draft, -1)
    frame_loss = (live_rows * divergence - LAM * picked).reshape(1, 1, block_rows)
    block_grad = (
        live_rows[:, None] * (draft_prob - target_prob) + LAM * (draft_prob - onehot)
    ).astype(jnp.bfloat16)
    returned = block_grad.reshape(block_rows, per_book, slice_cols).transpose(1, 0, 2)
    returned = regroup(
        returned, bit_total, lambda piece_data, bit_number: partner(piece_data, "voc", bit_number)
    )
    logit_grad = returned.reshape(row_count, slice_cols)
    act_part = inner_cols(logit_grad, vocab_proj)
    proj_grad = lax.psum(inner_rows(activation, logit_grad), "grp").astype(jnp.bfloat16)
    up_part = inner_cols(proj_grad, head_weight)
    act_grad = lax.psum(act_part, "voc")
    grad_b = lax.psum(up_part, "voc")
    pre_grad = (act_grad * silu_slope(pre_act)).astype(jnp.bfloat16)
    grad_a = lax.psum(inner_rows(hidden_states, pre_grad), "grp")
    return (frame_loss, grad_a, grad_b)


def solution(mesh):
    in_specs = (
        P("grp", "voc"),
        P("grp", "voc"),
        P("grp", None),
        P("voc", None),
        P(None, "grp"),
        P("grp", "voc"),
    )
    out_specs = (P("voc", "grp", None), P("voc", None), P(None, "grp"))
    return jax.shard_map(
        on_device, mesh=mesh, in_specs=in_specs, out_specs=out_specs, check_vma=False
    )
```

profile of v0, /device:TPU:2, one launch (start us, length us, event | category | flops | bytes accessed | tf_op | source)
XLA Modules:
  0.0 595.0 jit_solution(6902269092445431331)
XLA Ops:
  7.2 1.0 copy-done
  8.2 2.2 fusion.24
  10.4 0.0 all-reduce.11.cloned.1.call-start
  10.5 1.3 collective-permute-start
  11.8 2.0 fusion.25
  13.9 69.8 %all-reduce.12 = bf16[256,512]{1,0:T(8,128)(2,1)S(1)} all-reduce(f32[256,512]{1,0:T(8,128)} %fusion.25), channel_id=1, replica_groups=mesh['grp'=16,'voc'=32] {'grp'}, use_global_device_ids=true, to_apply=%region_1.2 | all-reduce | flops 131072 | bytes 786432 | tf_op jit(solution)/shard_map/psum | solution.py:80
  83.6 1.6 slice.38
  85.3 1.8 pad_maximum_fusion.2
  87.0 64.4 %all-reduce.7.cloned.1.call-done = f32[1024,256]{1,0:T(8,128)} async-done(((f32[1024,256]{1,0:T(8,128)}), f32[1024,256]{1,0:T(8,128)}) %all-reduce.7.cloned.1.call-update) | async-done | bytes 1048592 | tf_op jit(solution)/shard_map/psum | solution.py:76
  151.5 2.4 convolution_add_fusion
  153.9 1.9 select_bitcast_fusion.5
  155.8 2.0 collective-permute-start.1
  157.9 4.3 collective-permute-done.1
  162.2 3.4 select_bitcast_fusion.4
  165.6 0.4 maximum_bitcast_fusion
  166.1 0.5 select_bitcast_fusion.2
  166.6 1.5 copy-done.1
  168.1 2.5 collective-permute-start.2
  170.6 0.8 dynamic_slice.7
  171.4 46.4 %collective-permute-done.2 = f32[2,1,2,256,512]{4,3,0,2,1:T(8,128)} collective-permute-done((f32[2,1,2,256,512]{4,3,0,2,1:T(8,128)S(1)}, f32[2,1,2,256,512]{4,3,0,2,1:T(8,128)}, u32[]{:S(2)}, u32[]{:S(2)}) %collective-permute-start.2) | collective-permute-done | bytes 2097184 | tf_op jit(solution)/shard_map/ppermute | solution.py:19
  217.7 3.6 select_bitcast_fusion.1
  221.4 0.5 pad_maximum_fusion
  221.9 0.2 bitcast_reduce_fusion
  222.1 0.2 slice_reduce_fusion
  222.2 0.7 exponential_reduce_fusion.1
  223.0 1.0 multiply_reduce_fusion
  224.0 0.6 multiply_subtract_fusion
  224.6 1.6 fusion.6
  226.2 0.1 fusion.12
  226.2 1.9 collective-permute-start.3
  228.2 1.9 collective-permute-done.3
  230.0 0.1 select_bitcast_fusion.9
  230.2 0.1 maximum_bitcast_fusion.1
  230.3 0.1 fusion.13
  230.3 2.5 collective-permute-start.4
  232.8 13.4 %collective-permute-done.4 = bf16[1,2,256,512]{3,2,1,0:T(8,128)(2,1)S(1)} collective-permute-done((bf16[1,2,256,512]{3,2,1,0:T(8,128)(2,1)S(1)}, bf16[1,2,256,512]{3,2,1,0:T(8,128)(2,1)S(1)}, u32[]{:S(2)}, u32[]{:S(2)}) %collective-permute-start.4) | collective-permute-done | bytes 524320 | tf_op jit(solution)/shard_map/ppermute | solution.py:19
  246.2 0.1 select_bitcast_fusion.7
  246.3 0.1 pad_maximum_fusion.3
  246.4 1.5 fusion.27
  247.9 0.5 fusion.23
  248.4 63.2 %all-reduce.13 = bf16[256,512]{1,0:T(8,128)(2,1)S(1)} all-reduce(f32[256,512]{1,0:T(8,128)S(1)} %fusion.23), channel_id=1, replica_groups=mesh['grp'=16,'voc'=32] {'grp'}, use_global_device_ids=true, to_apply=%region_10.11 | all-reduce | flops 131072 | bytes 786432 | tf_op jit(solution)/shard_map/psum | solution.py:115
  311.6 1.1 fusion.26
  312.7 0.0 all-reduce.9.cloned.1.call-start
  312.8 133.0 %all-reduce.11.cloned.1.call-done = (f32[1024,256]{1,0:T(8,128)}, f32[256,512]{1,0:T(8,128)}) async-done(((f32[1024,256]{1,0:T(8,128)}, f32[256,512]{1,0:T(8,128)}), (f32[1024,256]{1,0:T(8,128)}, f32[256,512]{1,0:T(8,128)})) %all-reduce.11.cloned.1.call-update) | async-done | bytes 1572880 | tf_op jit(solution)/shard_map/psum | solution.py:117
  445.8 2.6 convolution_bitcast_fusion
  448.4 137.5 %all-reduce.9.cloned.1.call-done = f32[256,256]{0,1:T(8,128)} async-done(((f32[256,256]{0,1:T(8,128)}), f32[256,256]{0,1:T(8,128)}) %all-reduce.9.cloned.1.call-update) | async-done | bytes 262160 | tf_op jit(solution)/shard_map/psum | solution.py:120
  585.9 1.8 copy.27
  587.7 0.8 copy.41
  (22 shorter events, 0.1 us)
Async XLA Ops:
  7.2 1.0 copy-start
  7.2 3.3 copy-start.3
  7.2 4.6 copy-start.4
  7.2 144.3 %all-reduce.7.cloned.1.call-start = ((), (), s32[]{:S(2)}) async-start(), calls=%async_computation | async-start | bytes 2097152 | tf_op jit(solution)/shard_map/psum | solution.py:76
  10.4 435.4 %all-reduce.11.cloned.1.call-start = ((), (), s32[]{:S(2)}) async-start(), calls=%async_computation.2 | async-start | bytes 3145728 | tf_op jit(solution)/shard_map/psum | solution.py:117
  10.5 74.8 %collective-permute-start = (f32[2,512]{1,0:T(2,128)S(1)}, f32[2,512]{1,0:T(2,128)S(1)}, u32[]{:S(2)}, u32[]{:S(2)}) collective-permute-start(f32[2,512]{1,0:T(2,128)S(1)} %slice.39), channel_id=1, source_target_pairs={{32,0},{64,32},{96,64},{128,96},{160,128},{192,160},{224,192},{256... | collective-permute-start | bytes 12296 | tf_op jit(solution)/shard_map/ppermute | solution.py:13
  153.9 2.0 copy-start.2
  155.8 6.4 %collective-permute-start.1 = (f32[2,2,1,256,512]{4,3,1,0,2:T(8,128)}, f32[2,2,1,256,512]{4,3,1,0,2:T(8,128)}, u32[]{:S(2)}, u32[]{:S(2)}) collective-permute-start(f32[2,2,1,256,512]{4,3,1,0,2:T(8,128)} %select_bitcast_fusion.5), channel_id=1, source_target_pairs={{0,1},{1,0},{2,3},{3,2},{4,5},{5,4},{6,7},{7,6},{8,9},{9,8},{10,11... | collective-permute-start | bytes 6291464 | tf_op jit(solution)/shard_map/ppermute | solution.py:19
  166.1 2.0 copy-start.1
  168.1 49.7 %collective-permute-start.2 = (f32[2,1,2,256,512]{4,3,0,2,1:T(8,128)S(1)}, f32[2,1,2,256,512]{4,3,0,2,1:T(8,128)}, u32[]{:S(2)}, u32[]{:S(2)}) collective-permute-start(f32[2,1,2,256,512]{4,3,0,2,1:T(8,128)S(1)} %select_bitcast_fusion.2), channel_id=1, source_target_pairs={{0,2},{1,3},{2,0},{3,1},{4,6},{5,7},{6,4},{7,5},{8,10},{9,11},{10,... | collective-permute-start | bytes 6291464 | tf_op jit(solution)/shard_map/ppermute | solution.py:19
  226.2 3.8 collective-permute-start.3
  230.3 15.9 %collective-permute-start.4 = (bf16[1,2,256,512]{3,2,1,0:T(8,128)(2,1)S(1)}, bf16[1,2,256,512]{3,2,1,0:T(8,128)(2,1)S(1)}, u32[]{:S(2)}, u32[]{:S(2)}) collective-permute-start(bf16[1,2,256,512]{3,2,1,0:T(8,128)(2,1)S(1)} %fusion.13), channel_id=1, source_target_pairs={{0,2},{1,3},{2,0},{3,1},{4,6},{5,7},{6,4},{7,5},{8,10},{9,11},{10,... | collective-permute-start | bytes 1572872 | tf_op jit(solution)/shard_map/ppermute | solution.py:19
  246.3 1.6 copy-start.6
  312.7 273.1 %all-reduce.9.cloned.1.call-start = ((), (), s32[]{:S(2)}) async-start(), calls=%async_computation.1 | async-start | bytes 524288 | tf_op jit(solution)/shard_map/psum | solution.py:120
  445.8 141.9 %copy-start.5 = (f32[256,512]{1,0:T(8,128)S(1)}, f32[256,512]{1,0:T(8,128)}, u32[]{:S(2)}) copy-start(f32[256,512]{1,0:T(8,128)} %get-tuple-element.24) | copy-start | bytes 1572868
Sparse Core Ops, SparseCore 0:
  11.2 140.2 all-reduce.6
  312.8 132.9 all-reduce.10
  448.7 137.1 all-reduce.8
where the time goes:
time: 595 us
  waiting for transfers between devices  401 us (67%)
  blocking collectives  133 us (22%)
  other arithmetic  17 us (3%)
  between operations  14.1 us (2%)
  matrix products  12.3 us (2%)
  starting transfers between devices  10.3 us (2%)
  local copies, waits for them, and re-layouts  7.43 us (1%)
    psum x1, waiting for transfers between devices, on_device(): grad_a = lax.psum(inner_rows(hidden_states, pre_grad), 'grp')  137 us
    psum x1, waiting for transfers between devices, on_device(): act_grad = lax.psum(act_part, 'voc')  133 us
    psum x1, blocking collectives, on_device(): lax.psum(jnp.dot(up_weight, head_weight, preferred_element_type=jnp.float...  69.8 us
    ppermute x4, waiting for transfers between devices, partner(): return lax.ppermute(value, axis, pairs)  66 us
    psum x1, waiting for transfers between devices, on_device(): lax.psum(jnp.dot(hidden_states, down_weight, preferred_element_type=jnp.f...  64.4 us
    psum x1, blocking collectives, on_device(): lax.psum(inner_rows(activation, logit_grad), 'grp').astype(jnp.bfloat16)  63.2 us
  transfers between devices with their start and end apart: 8, of which 7 were waited for; matrix products, arithmetic and copies ran while one was open for 1% of the time, Pallas kernels for 0%

commit v1 on v0

--- a/solution.py
+++ b/solution.py
@@ -114,7 +114,9 @@
     act_part = inner_cols(logit_grad, vocab_proj)
     proj_grad = lax.psum(inner_rows(activation, logit_grad), "grp").astype(jnp.bfloat16)
     up_part = inner_cols(proj_grad, head_weight)
-    act_grad = lax.psum(act_part, "voc")
+    act_grad = act_part
+    for hop in (1, 2, 4, 8, 16):
+        act_grad = act_grad + lax.ppermute(act_grad, "voc", [(dev, dev ^ hop) for dev in range(32)])
     grad_b = lax.psum(up_part, "voc")
     pre_grad = (act_grad * silu_slope(pre_act)).astype(jnp.bfloat16)
     grad_a = lax.psum(inner_rows(hidden_states, pre_grad), "grp")

time: 595 us -> 643 us (1.081)
  the two profiles are of different devices: /device:TPU:2 before, /device:TPU:1 now
where the time goes in v1:
time: 643 us; the launch traced here: 642 us
  waiting for transfers between devices  453 us (70%)
  blocking collectives  109 us (17%)
  starting transfers between devices  29.7 us (5%)
  other arithmetic  17.6 us (3%)
  between operations  14.1 us (2%)
  matrix products  9.98 us (2%)
  local copies, waits for them, and re-layouts  8.5 us (1%)
    psum x1, waiting for transfers between devices, on_device(): grad_b = lax.psum(up_part, 'voc')  143 us
    ppermute x5, waiting for transfers between devices, on_device(): lax.ppermute(act_grad, 'voc', [(dev, dev ^ hop) for dev in range(32)])  90.7 us
    psum x1, waiting for transfers between devices, on_device(): grad_a = lax.psum(inner_rows(hidden_states, pre_grad), 'grp')  78 us
    psum x1, waiting for transfers between devices, on_device(): lax.psum(jnp.dot(hidden_states, down_weight, preferred_element_type=jnp.f...  77.6 us
    ppermute x4, waiting for transfers between devices, partner(): return lax.ppermute(value, axis, pairs)  63.6 us
    psum x1, blocking collectives, on_device(): lax.psum(jnp.dot(up_weight, head_weight, preferred_element_type=jnp.float...  58 us
    psum x1, blocking collectives, on_device(): lax.psum(inner_rows(activation, logit_grad), 'grp').astype(jnp.bfloat16)  51.1 us
    ppermute x5, starting transfers between devices, on_device(): lax.ppermute(act_grad, 'voc', [(dev, dev ^ hop) for dev in range(32)])  17.6 us
  transfers between devices with their start and end apart: 13, of which 12 were waited for; matrix products, arithmetic and copies ran while one was open for 2% of the time, Pallas kernels for 0%

profile of v1, /device:TPU:1, one launch (start us, length us, event | category | flops | bytes accessed | tf_op | source)
XLA Modules:
  0.0 642.2 jit_solution(14458993562253109754)
XLA Ops:
  7.2 1.0 copy-done
  8.2 2.2 fusion.24
  10.5 1.3 collective-permute-start
  11.8 2.0 fusion.25
  13.8 58.0 %all-reduce.11 = bf16[256,512]{1,0:T(8,128)(2,1)S(1)} all-reduce(f32[256,512]{1,0:T(8,128)} %fusion.25), channel_id=1, replica_groups=mesh['grp'=16,'voc'=32] {'grp'}, use_global_device_ids=true, to_apply=%region_1.2 | all-reduce | flops 131072 | bytes 786432 | tf_op jit(solution)/shard_map/psum | solution.py:80
  71.9 1.6 slice.38
  73.5 1.8 pad_maximum_fusion.2
  75.3 77.6 %all-reduce.6.cloned.1.call-done = f32[1024,256]{1,0:T(8,128)} async-done(((f32[1024,256]{1,0:T(8,128)}), f32[1024,256]{1,0:T(8,128)}) %all-reduce.6.cloned.1.call-update) | async-done | bytes 1048592 | tf_op jit(solution)/shard_map/psum | solution.py:76
  152.8 2.4 convolution_add_fusion
  155.2 1.9 select_bitcast_fusion.5
  157.2 2.6 collective-permute-start.1
  159.9 4.1 collective-permute-done.1
  163.9 3.4 select_bitcast_fusion.4
  167.3 0.4 maximum_bitcast_fusion
  167.8 0.5 select_bitcast_fusion.2
  168.3 1.5 copy-done.1
  169.8 2.5 collective-permute-start.2
  172.3 0.8 dynamic_slice.7
  173.1 45.5 %collective-permute-done.2 = f32[2,1,2,256,512]{4,3,0,2,1:T(8,128)} collective-permute-done((f32[2,1,2,256,512]{4,3,0,2,1:T(8,128)S(1)}, f32[2,1,2,256,512]{4,3,0,2,1:T(8,128)}, u32[]{:S(2)}, u32[]{:S(2)}) %collective-permute-start.2) | collective-permute-done | bytes 2097184 | tf_op jit(solution)/shard_map/ppermute | solution.py:19
  218.6 3.6 select_bitcast_fusion.1
  222.2 0.5 pad_maximum_fusion
  223.1 0.7 exponential_reduce_fusion.1
  223.8 1.0 multiply_reduce_fusion
  224.8 0.6 multiply_subtract_fusion
  225.5 1.6 fusion.6
  227.1 3.1 collective-permute-start.3
  230.2 1.5 collective-permute-done.3
  232.0 2.5 collective-permute-start.4
  234.5 12.5 %collective-permute-done.4 = bf16[1,2,256,512]{3,2,1,0:T(8,128)(2,1)S(1)} collective-permute-done((bf16[1,2,256,512]{3,2,1,0:T(8,128)(2,1)S(1)}, bf16[1,2,256,512]{3,2,1,0:T(8,128)(2,1)S(1)}, u32[]{:S(2)}, u32[]{:S(2)}) %collective-permute-start.4) | collective-permute-done | bytes 524320 | tf_op jit(solution)/shard_map/ppermute | solution.py:19
  247.3 0.5 fusion.27
  247.7 3.1 collective-permute-start.5
  250.9 2.3 collective-permute-done.5
  253.3 2.5 collective-permute-start.6
  255.8 23.8 %collective-permute-done.6 = f32[1024,256]{1,0:T(8,128)S(1)} collective-permute-done((f32[1024,256]{1,0:T(8,128)S(1)}, f32[1024,256]{1,0:T(8,128)S(1)}, u32[]{:S(2)}, u32[]{:S(2)}) %collective-permute-start.6) | collective-permute-done | bytes 1048608 | tf_op jit(solution)/shard_map/ppermute | solution.py:119
  279.7 4.2 collective-permute-start.7
  283.9 22.7 %collective-permute-done.7 = f32[1024,256]{1,0:T(8,128)S(1)} collective-permute-done((f32[1024,256]{1,0:T(8,128)S(1)}, f32[1024,256]{1,0:T(8,128)S(1)}, u32[]{:S(2)}, u32[]{:S(2)}) %collective-permute-start.7) | collective-permute-done | bytes 1048608 | tf_op jit(solution)/shard_map/ppermute | solution.py:119
  306.7 2.7 collective-permute-start.8
  309.4 22.0 %collective-permute-done.8 = f32[1024,256]{1,0:T(8,128)S(1)} collective-permute-done((f32[1024,256]{1,0:T(8,128)S(1)}, f32[1024,256]{1,0:T(8,128)S(1)}, u32[]{:S(2)}, u32[]{:S(2)}) %collective-permute-start.8) | collective-permute-done | bytes 1048608 | tf_op jit(solution)/shard_map/ppermute | solution.py:119
  331.5 5.1 collective-permute-start.9
  336.6 0.5 fusion.23
  337.2 20.1 %collective-permute-done.9 = f32[1024,256]{1,0:T(8,128)S(1)} collective-permute-done((f32[1024,256]{1,0:T(8,128)S(1)}, f32[1024,256]{1,0:T(8,128)S(1)}, u32[]{:S(2)}, u32[]{:S(2)}) %collective-permute-start.9) | collective-permute-done | bytes 1048608 | tf_op jit(solution)/shard_map/ppermute | solution.py:119
  357.2 1.3 convolution_bitcast_fusion
  358.6 51.1 %all-reduce.12 = bf16[256,512]{1,0:T(8,128)(2,1)S(1)} all-reduce(f32[256,512]{1,0:T(8,128)S(1)} %fusion.23), channel_id=1, replica_groups=mesh['grp'=16,'voc'=32] {'grp'}, use_global_device_ids=true, to_apply=%region_9.10 | all-reduce | flops 131072 | bytes 786432 | tf_op jit(solution)/shard_map/psum | solution.py:115
  409.6 1.1 fusion.26
  410.8 78.0 %all-reduce.8.cloned.1.call-done = f32[256,256]{0,1:T(8,128)} async-done(((f32[256,256]{0,1:T(8,128)}), f32[256,256]{0,1:T(8,128)}) %all-reduce.8.cloned.1.call-update) | async-done | bytes 262160 | tf_op jit(solution)/shard_map/psum | solution.py:122
  488.8 1.8 copy.27
  490.6 143.3 %all-reduce.10.cloned.1.call-done = f32[256,512]{1,0:T(8,128)} async-done(((f32[256,512]{1,0:T(8,128)}), f32[256,512]{1,0:T(8,128)}) %all-reduce.10.cloned.1.call-update) | async-done | bytes 524304 | tf_op jit(solution)/shard_map/psum | solution.py:120
  633.8 1.9 copy.40
  (34 shorter events, 1.7 us)
Async XLA Ops:
  7.2 1.0 copy-start
  7.2 3.3 copy-start.3
  7.2 4.6 copy-start.4
  7.2 145.6 %all-reduce.6.cloned.1.call-start = ((), (), s32[]{:S(2)}) async-start(), calls=%async_computation | async-start | bytes 2097152 | tf_op jit(solution)/shard_map/psum | solution.py:76
  10.4 478.4 %all-reduce.8.cloned.1.call-start = ((), (), s32[]{:S(2)}) async-start(), calls=%async_computation.1 | async-start | bytes 524288 | tf_op jit(solution)/shard_map/psum | solution.py:122
  10.5 63.0 %collective-permute-start = (f32[2,512]{1,0:T(2,128)S(1)}, f32[2,512]{1,0:T(2,128)S(1)}, u32[]{:S(2)}, u32[]{:S(2)}) collective-permute-start(f32[2,512]{1,0:T(2,128)S(1)} %slice.39), channel_id=1, source_target_pairs={{32,0},{64,32},{96,64},{128,96},{160,128},{192,160},{224,192},{256... | collective-permute-start | bytes 12296 | tf_op jit(solution)/shard_map/ppermute | solution.py:13
  155.2 2.0 copy-start.2
  157.2 6.7 %collective-permute-start.1 = (f32[2,2,1,256,512]{4,3,1,0,2:T(8,128)}, f32[2,2,1,256,512]{4,3,1,0,2:T(8,128)}, u32[]{:S(2)}, u32[]{:S(2)}) collective-permute-start(f32[2,2,1,256,512]{4,3,1,0,2:T(8,128)} %select_bitcast_fusion.5), channel_id=1, source_target_pairs={{0,1},{1,0},{2,3},{3,2},{4,5},{5,4},{6,7},{7,6},{8,9},{9,8},{10,11... | collective-permute-start | bytes 6291464 | tf_op jit(solution)/shard_map/ppermute | solution.py:19
  167.8 2.0 copy-start.1
  169.8 48.8 %collective-permute-start.2 = (f32[2,1,2,256,512]{4,3,0,2,1:T(8,128)S(1)}, f32[2,1,2,256,512]{4,3,0,2,1:T(8,128)}, u32[]{:S(2)}, u32[]{:S(2)}) collective-permute-start(f32[2,1,2,256,512]{4,3,0,2,1:T(8,128)S(1)} %select_bitcast_fusion.2), channel_id=1, source_target_pairs={{0,2},{1,3},{2,0},{3,1},{4,6},{5,7},{6,4},{7,5},{8,10},{9,11},{10,... | collective-permute-start | bytes 6291464 | tf_op jit(solution)/shard_map/ppermute | solution.py:19
  227.1 4.7 collective-permute-start.3
  232.0 15.0 %collective-permute-start.4 = (bf16[1,2,256,512]{3,2,1,0:T(8,128)(2,1)S(1)}, bf16[1,2,256,512]{3,2,1,0:T(8,128)(2,1)S(1)}, u32[]{:S(2)}, u32[]{:S(2)}) collective-permute-start(bf16[1,2,256,512]{3,2,1,0:T(8,128)(2,1)S(1)} %fusion.13), channel_id=1, source_target_pairs={{0,2},{1,3},{2,0},{3,1},{4,6},{5,7},{6,4},{7,5},{8,10},{9,11},{10,... | collective-permute-start | bytes 1572872 | tf_op jit(solution)/shard_map/ppermute | solution.py:19
  247.7 5.4 collective-permute-start.5
  253.3 26.2 %collective-permute-start.6 = (f32[1024,256]{1,0:T(8,128)S(1)}, f32[1024,256]{1,0:T(8,128)S(1)}, u32[]{:S(2)}, u32[]{:S(2)}) collective-permute-start(f32[1024,256]{1,0:T(8,128)S(1)} %add.83), channel_id=1, source_target_pairs={{0,2},{1,3},{2,0},{3,1},{4,6},{5,7},{6,4},{7,5},{8,10},{9,11},{10,... | collective-permute-start | bytes 3145736 | tf_op jit(solution)/shard_map/ppermute | solution.py:119
  279.7 26.9 %collective-permute-start.7 = (f32[1024,256]{1,0:T(8,128)S(1)}, f32[1024,256]{1,0:T(8,128)S(1)}, u32[]{:S(2)}, u32[]{:S(2)}) collective-permute-start(f32[1024,256]{1,0:T(8,128)S(1)} %add.84), channel_id=1, source_target_pairs={{0,4},{1,5},{2,6},{3,7},{4,0},{5,1},{6,2},{7,3},{8,12},{9,13},{10,... | collective-permute-start | bytes 3145736 | tf_op jit(solution)/shard_map/ppermute | solution.py:119
  306.7 30.0 %copy-start.5 = (f32[1024,256]{1,0:T(8,128)S(1)}, f32[1024,256]{1,0:T(8,128)}, u32[]{:S(2)}) copy-start(f32[1024,256]{1,0:T(8,128)} %all-reduce.6.cloned.1.call-done) | copy-start | bytes 3145732
  306.7 24.7 %collective-permute-start.8 = (f32[1024,256]{1,0:T(8,128)S(1)}, f32[1024,256]{1,0:T(8,128)S(1)}, u32[]{:S(2)}, u32[]{:S(2)}) collective-permute-start(f32[1024,256]{1,0:T(8,128)S(1)} %add.85), channel_id=1, source_target_pairs={{0,8},{1,9},{2,10},{3,11},{4,12},{5,13},{6,14},{7,15},{8,0},{9,1},... | collective-permute-start | bytes 3145736 | tf_op jit(solution)/shard_map/ppermute | solution.py:119
  331.5 25.7 %collective-permute-start.9 = (f32[1024,256]{1,0:T(8,128)S(1)}, f32[1024,256]{1,0:T(8,128)S(1)}, u32[]{:S(2)}, u32[]{:S(2)}) collective-permute-start(f32[1024,256]{1,0:T(8,128)S(1)} %add.86), channel_id=1, source_target_pairs={{0,16},{1,17},{2,18},{3,19},{4,20},{5,21},{6,22},{7,23},{8,24},{9,... | collective-permute-start | bytes 3145736 | tf_op jit(solution)/shard_map/ppermute | solution.py:119
  358.5 275.3 %all-reduce.10.cloned.1.call-start = ((), (), s32[]{:S(2)}) async-start(), calls=%async_computation.2 | async-start | bytes 1048576 | tf_op jit(solution)/shard_map/psum | solution.py:120
Sparse Core Ops, SparseCore 0:
  11.2 141.5 all-reduce.5
  358.6 130.0 all-reduce.7
  492.5 141.2 all-reduce.9
